TPU v7x, 256 devices: a whole 4x4x8 slice. The times are simulated.
256 devices in a mesh: chan: 16 (over y, x_hi, core), win: 16 (over z, x_lo).
Axes of the slice: x: 4 (x_hi: 2, x_lo: 2; x = x_hi * 2 + x_lo), y: 4, z: 8, core: 2. Of those that a mesh axis runs over, the one named last changes fastest.
Arguments:
- spectra: bfloat16 [64, 512, 4096], P('win', 'chan'), may hold values from -80 to 80
- quality: int32 [512], P('chan'), may hold values 0 or 1
- source_block: int32 [2], replicated, may hold values from 0 to 63
Outputs:
- correlations: bfloat16 [2, 512, 8, 512], P(None, ('chan', 'win'))
All inputs are finite; a program needn't handle non-finite values. No bound on the sum of `quality` on one device may be relied on, other than what follows from the above.
Results may differ from a plain program's by a relative error of at most 0.0045.
Values may be sent and summed in bfloat16 or wider, within the bound.
A program may use at most 192 MiB of HBM per device.

v0:
```python
import math
import jax
import jax.numpy as jnp
from jax import lax
from jax.sharding import PartitionSpec as P

L = 512
SRC = 8
STEPS = 2


def from_root(value, axis, source):
    kept = jnp.where(lax.axis_index(axis) == source, value, 0).astype(value.dtype)
    return lax.psum(kept, axis)


def lag_table(bins, lags, factor):
    bin_index = lax.iota(jnp.int32, bins)[:, None]
    shifts = lax.iota(jnp.int32, lags)[None, :] - lags // 2
    residue = jnp.mod(bin_index * shifts, 2 * bins)
    phase_angle = residue.astype(jnp.float32) * (2.0 * math.pi / (2 * bins))
    return jnp.concatenate([jnp.cos(phase_angle), -jnp.sin(phase_angle)], axis=0) * factor


def whiten(block, quality):
    values = block.astype(jnp.float32)
    bins = values.shape[-1] // 2
    energy = jnp.sum(values * values, axis=-1) / bins
    weights = quality.astype(jnp.float32)[None, :] / jnp.sqrt(energy + 1e-06)
    return (values * weights[:, :, None]).astype(jnp.bfloat16)


def cross_spectra(sources, receivers):
    bins = sources.shape[-1] // 2
    src_real = sources[:, :, :bins]
    src_imag = sources[:, :, bins:]
    rec_real = receivers[:, :, :bins]
    rec_imag = receivers[:, :, bins:]
    real_part = jnp.einsum("wsf,wrf->rsf", src_real, rec_real, preferred_element_type=jnp.float32)
    real_part = real_part + jnp.einsum(
        "wsf,wrf->rsf", src_imag, rec_imag, preferred_element_type=jnp.float32
    )
    imag_part = jnp.einsum("wsf,wrf->rsf", src_real, rec_imag, preferred_element_type=jnp.float32)
    imag_part = imag_part - jnp.einsum(
        "wsf,wrf->rsf", src_imag, rec_real, preferred_element_type=jnp.float32
    )
    return jnp.concatenate([real_part, imag_part], axis=-1)


def apply_lags(cross, transform):
    lagged = jnp.dot(
        cross.reshape(-1, cross.shape[-1]),
        transform,
        precision=lax.Precision.HIGHEST,
        preferred_element_type=jnp.float32,
    )
    return lagged.reshape(cross.shape[0], cross.shape[1], transform.shape[1])


def body(spectra, quality, source_block):
    window_count, channel_count, row_width = spectra.shape
    bins = row_width // 2
    total_windows = window_count * lax.axis_size("win")
    transform = lag_table(bins, L, 1.0 / math.sqrt(row_width * total_windows))
    whitened = whiten(spectra, quality)
    per_group = channel_count // SRC
    results = []
    for step in range(STEPS):
        block_index = source_block[step]
        root_group = block_index // per_group
        offset = block_index % per_group * SRC
        own_block = lax.dynamic_slice_in_dim(whitened, offset, SRC, 1)
        sources = from_root(own_block, "chan", root_group)
        partial_cross = cross_spectra(sources, whitened)
        stacked = lax.psum_scatter(partial_cross, "win", scatter_dimension=0, tiled=True)
        lagged = apply_lags(stacked, transform)
        results.append(lagged.astype(jnp.bfloat16))
    return jnp.stack(results)


def solution(mesh):
    return jax.shard_map(
        body,
        mesh=mesh,
        in_specs=(P("win", "chan", None), P("chan"), P()),
        out_specs=P(None, ("chan", "win"), None, None),
        check_vma=False,
    )
```

profile of v0, /device:TPU:8, one launch (start us, length us, event | category | flops | bytes accessed | tf_op | source)
XLA Modules:
  0.0 444.0 jit_solution(556799293227208969)
XLA Ops:
  13.1 1.5 fusion.13
  17.8 2.5 copy.4
  21.7 136.2 %all-reduce.3.cloned.1.call-done = (bf16[4,8,4096]{2,1,0:T(8,128)(2,1)}, bf16[4,8,4096]{2,1,0:T(8,128)(2,1)}) async-done(((bf16[4,8,4096]{2,1,0:T(8,128)(2,1)}, bf16[4,8,4096]{2,1,0:T(8,128)(2,1)}), (bf16[4,8,4096]{2,1,0:T(8,128)(2,1)}, bf16[4,8,4096]{2,1,0:T(8,128)(2,1)})) %all-reduce.3.cloned.1.call-update) | async-done | bytes 524304 | tf_op jit(solution)/shard_map/psum | solution.py:14
  159.0 2.4 copy.5
  161.5 2.4 copy.8
  163.9 7.4 %fusion.36 = f32[2048,32,8]{1,2,0:T(8,128)} fusion(bf16[4,32,2048]{1,0,2:T(4,128)(2,1)} %copy.4, bf16[4,8,2048]{1,0,2:T(4,128)(2,1)} %copy.5), kind=kOutput, calls=%fused_computation.44 | convolution fusion | flops 4194304 | bytes 2752512 | tf_op jit(solution)/shard_map/wsf,wrf->rsf/dot_general | solution.py:39
  171.3 4.8 %fusion.38 = f32[2048,32,8]{1,2,0:T(8,128)} fusion(bf16[4,32,2048]{1,0,2:T(4,128)(2,1)S(1)} %copy.7, bf16[4,8,2048]{1,0,2:T(4,128)(2,1)S(1)} %copy-done.2), kind=kOutput, calls=%fused_computation.46 | convolution fusion | flops 4194304 | bytes 2752512 | tf_op jit(solution)/shard_map/wsf,wrf->rsf/dot_general | solution.py:43
  176.1 4.8 %fusion.37 = f32[2048,32,8]{1,2,0:T(8,128)} fusion(bf16[4,32,2048]{1,0,2:T(4,128)(2,1)S(1)} %copy.7, bf16[4,8,2048]{1,0,2:T(4,128)(2,1)S(1)} %copy-done.1), kind=kOutput, calls=%fused_computation.45 | convolution fusion | flops 4194304 | bytes 2752512 | tf_op jit(solution)/shard_map/wsf,wrf->rsf/dot_general | solution.py:40
  180.9 4.8 %fusion.39 = f32[2048,32,8]{1,2,0:T(8,128)} fusion(bf16[4,32,2048]{1,0,2:T(4,128)(2,1)S(1)} %copy-done, bf16[4,8,2048]{1,0,2:T(4,128)(2,1)S(1)} %copy-done.1), kind=kOutput, calls=%fused_computation.47 | convolution fusion | flops 4194304 | bytes 2752512 | tf_op jit(solution)/shard_map/wsf,wrf->rsf/dot_general | solution.py:44
  185.7 6.7 %copy.6 = f32[2048,32,8]{0,2,1:T(8,128)} copy(f32[2048,32,8]{1,2,0:T(8,128)} %fusion.36) | data formatting | bytes 4194304 | tf_op jit(solution)/shard_map/wsf,wrf->rsf/dot_general | solution.py:39
  192.3 6.6 %copy.9 = f32[2048,32,8]{0,2,1:T(8,128)} copy(f32[2048,32,8]{1,2,0:T(8,128)} %fusion.37) | data formatting | bytes 4194304 | tf_op jit(solution)/shard_map/wsf,wrf->rsf/dot_general | solution.py:40
  198.9 6.6 %copy.10 = f32[2048,32,8]{0,2,1:T(8,128)} copy(f32[2048,32,8]{1,2,0:T(8,128)} %fusion.38) | data formatting | bytes 4194304 | tf_op jit(solution)/shard_map/wsf,wrf->rsf/dot_general | solution.py:43
  205.6 6.6 %copy.11 = f32[2048,32,8]{0,2,1:T(8,128)} copy(f32[2048,32,8]{1,2,0:T(8,128)} %fusion.39) | data formatting | bytes 4194304 | tf_op jit(solution)/shard_map/wsf,wrf->rsf/dot_general | solution.py:44
  212.2 2.7 add_bitcast_fusion.1
  215.9 2.4 pad_maximum_fusion
  218.6 2.5 copy.12
  221.1 7.2 %fusion.40 = f32[2048,32,8]{1,2,0:T(8,128)} fusion(bf16[4,32,2048]{1,0,2:T(4,128)(2,1)} %copy.4, bf16[4,8,2048]{1,0,2:T(4,128)(2,1)} %copy.12), kind=kOutput, calls=%fused_computation.48 | convolution fusion | flops 4194304 | bytes 2752512 | tf_op jit(solution)/shard_map/wsf,wrf->rsf/dot_general | solution.py:39
  228.3 6.6 %copy.13 = f32[2048,32,8]{0,2,1:T(8,128)} copy(f32[2048,32,8]{1,2,0:T(8,128)} %fusion.40) | data formatting | bytes 4194304 | tf_op jit(solution)/shard_map/wsf,wrf->rsf/dot_general | solution.py:39
  234.9 2.4 copy.14
  237.3 6.1 %fusion.41 = f32[2048,32,8]{1,2,0:T(8,128)} fusion(bf16[4,32,2048]{1,0,2:T(4,128)(2,1)S(1)} %copy.7, bf16[4,8,2048]{1,0,2:T(4,128)(2,1)} %copy.14), kind=kOutput, calls=%fused_computation.49 | convolution fusion | flops 4194304 | bytes 2752512 | tf_op jit(solution)/shard_map/wsf,wrf->rsf/dot_general | solution.py:40
  243.4 6.6 %copy.15 = f32[2048,32,8]{0,2,1:T(8,128)} copy(f32[2048,32,8]{1,2,0:T(8,128)} %fusion.41) | data formatting | bytes 4194304 | tf_op jit(solution)/shard_map/wsf,wrf->rsf/dot_general | solution.py:40
  250.0 7.2 %fusion.43 = f32[2048,32,8]{1,2,0:T(8,128)} fusion(bf16[4,32,2048]{1,0,2:T(4,128)(2,1)} %copy.4, bf16[4,8,2048]{1,0,2:T(4,128)(2,1)} %copy.14), kind=kOutput, calls=%fused_computation.51 | convolution fusion | flops 4194304 | bytes 2752512 | tf_op jit(solution)/shard_map/wsf,wrf->rsf/dot_general | solution.py:44
  257.2 6.7 %copy.17 = f32[2048,32,8]{0,2,1:T(8,128)} copy(f32[2048,32,8]{1,2,0:T(8,128)} %fusion.43) | data formatting | bytes 4194304 | tf_op jit(solution)/shard_map/wsf,wrf->rsf/dot_general | solution.py:44
  263.9 6.0 %fusion.42 = f32[2048,32,8]{1,2,0:T(8,128)} fusion(bf16[4,32,2048]{1,0,2:T(4,128)(2,1)S(1)} %copy.7, bf16[4,8,2048]{1,0,2:T(4,128)(2,1)} %copy.12), kind=kOutput, calls=%fused_computation.50 | convolution fusion | flops 4194304 | bytes 2752512 | tf_op jit(solution)/shard_map/wsf,wrf->rsf/dot_general | solution.py:43
  270.0 6.8 %copy.16 = f32[2048,32,8]{0,2,1:T(8,128)} copy(f32[2048,32,8]{1,2,0:T(8,128)} %fusion.42) | data formatting | bytes 4194304 | tf_op jit(solution)/shard_map/wsf,wrf->rsf/dot_general | solution.py:43
  276.8 2.0 add_bitcast_fusion
  279.9 2.4 pad_maximum_fusion.1
  282.4 18.0 %fusion.15 = (f32[2048,512]{1,0:T(8,128)}, f32[2048,512]{1,0:T(8,128)}) fusion(s32[512]{0:T(512)S(1)} %iota_add_fusion), kind=kLoop, calls=%fused_computation.24 | loop fusion | flops 15728640 | bytes 8390656 | tf_op jit(solution)/shard_map/cos | solution.py:22
  300.4 26.2 %reduce-scatter.3.cloned.1.call-done = f32[2,8,4096]{2,1,0:T(8,128)} async-done(((f32[32,8,4096]{2,1,0:T(8,128)}), f32[2,8,4096]{2,1,0:T(8,128)}) %reduce-scatter.3.cloned.1.call-update) | async-done | bytes 262160 | tf_op jit(solution)/shard_map/reduce_scatter | solution.py:75
  326.6 7.8 %fusion.25 = bf16[1,2,8,512]{3,2,1,0:T(8,128)(2,1)S(1)} fusion(f32[2,8,4096]{2,1,0:T(8,128)} %reduce-scatter.3.cloned.1.call-done, f32[2048,512]{1,0:T(8,128)} %get-tuple-element.16, f32[2048,512]{1,0:T(8,128)} %get-tuple-element.15), kind=kOutput, calls=%fused_computation.30 | convolution fusion | flops 406855680 | bytes 8667136 | tf_op jit(solution)/shard_map/dot_general | solution.py:51
  334.4 94.7 %reduce-scatter.5.cloned.1.call-done = f32[2,8,4096]{2,1,0:T(8,128)} async-done(((f32[32,8,4096]{2,1,0:T(8,128)}), f32[2,8,4096]{2,1,0:T(8,128)}) %reduce-scatter.5.cloned.1.call-update) | async-done | bytes 262160 | tf_op jit(solution)/shard_map/reduce_scatter | solution.py:75
  429.1 7.8 %fusion.22 = bf16[1,2,8,512]{3,2,1,0:T(8,128)(2,1)S(1)} fusion(f32[2,8,4096]{2,1,0:T(8,128)} %reduce-scatter.5.cloned.1.call-done, f32[2048,512]{1,0:T(8,128)} %get-tuple-element.16, f32[2048,512]{1,0:T(8,128)} %get-tuple-element.15), kind=kOutput, calls=%fused_computation.29 | convolution fusion | flops 406855680 | bytes 8667136 | tf_op jit(solution)/shard_map/dot_general | solution.py:51
  (34 shorter events, 10.1 us)
Async XLA Ops:
  6.5 151.4 %all-reduce.3.cloned.1.call-start = ((), (), s32[]{:S(2)}) async-start(), calls=%async_computation.4 | async-start | bytes 1048576 | tf_op jit(solution)/shard_map/psum | solution.py:14
  17.7 308.9 %reduce-scatter.3.cloned.1.call-start = ((), (), s32[]{:S(2)}) async-start(), calls=%async_computation.2 | async-start | bytes 4456448 | tf_op jit(solution)/shard_map/reduce_scatter | solution.py:75
  163.9 7.4 %copy-start.2 = (bf16[4,8,2048]{1,0,2:T(4,128)(2,1)S(1)}, bf16[4,8,2048]{1,0,2:T(4,128)(2,1)}, u32[]{:S(2)}) copy-start(bf16[4,8,2048]{1,0,2:T(4,128)(2,1)} %copy.5) | copy-start | bytes 393220
  171.3 4.8 %copy-start.1 = (bf16[4,8,2048]{1,0,2:T(4,128)(2,1)S(1)}, bf16[4,8,2048]{1,0,2:T(4,128)(2,1)}, u32[]{:S(2)}) copy-start(bf16[4,8,2048]{1,0,2:T(4,128)(2,1)} %copy.8) | copy-start | bytes 393220
  176.1 4.8 %copy-start = (bf16[4,32,2048]{1,0,2:T(4,128)(2,1)S(1)}, bf16[4,32,2048]{1,0,2:T(4,128)(2,1)}, u32[]{:S(2)}) copy-start(bf16[4,32,2048]{1,0,2:T(4,128)(2,1)} %copy.4) | copy-start | bytes 1572868
  212.2 2.9 copy-start.5
  212.2 3.5 copy-start.6
  218.4 210.7 %reduce-scatter.5.cloned.1.call-start = ((), (), s32[]{:S(2)}) async-start(), calls=%async_computation.3 | async-start | bytes 4456448 | tf_op jit(solution)/shard_map/reduce_scatter | solution.py:75
  270.0 6.8 %copy-start.3 = (f32[2048,32,8]{0,2,1:T(8,128)S(1)}, f32[2048,32,8]{0,2,1:T(8,128)}, u32[]{:S(2)}) copy-start(f32[2048,32,8]{0,2,1:T(8,128)} %copy.13) | copy-start | bytes 6291460
  276.8 2.2 copy-start.4
  276.8 2.9 copy-start.7
Sparse Core Ops, SparseCore 0:
  17.8 140.0 all-reduce.2
  218.5 108.0 reduce-scatter.2
  329.3 99.7 reduce-scatter.4
where the time goes:
time: 445 us; the launch traced here: 444 us
  waiting for transfers between devices  257 us (58%)
  local copies, waits for them, and re-layouts  71.1 us (16%)
  matrix products  63.9 us (14%)
  other arithmetic  33.3 us (7%)
  between operations  18.4 us (4%)
    psum x1, waiting for transfers between devices, from_root(): return lax.psum(kept, axis)  136 us
    reduce_scatter x2, waiting for transfers between devices, body(): lax.psum_scatter(partial_cross, 'win', scatter_dimension=0, tiled=True)  121 us
    cos x1, other arithmetic, lag_table(): jnp.cos(phase_angle)  18 us
    dot_general x2, matrix products, apply_lags(): jnp.dot(cross.reshape(-1, cross.shape[-1]), transform, precision=lax.Prec...  15.6 us
    dot_general x2, matrix products, cross_spectra(): jnp.einsum('wsf,wrf->rsf', src_real, rec_real, preferred_element_type=jnp...  14.6 us
    dot_general x2, local copies, waits for them, and re-layouts, cross_spectra(): jnp.einsum('wsf,wrf->rsf', src_real, rec_imag, preferred_element_type=jnp...  13.5 us
    dot_general x2, local copies, waits for them, and re-layouts, cross_spectra(): jnp.einsum('wsf,wrf->rsf', src_real, rec_real, preferred_element_type=jnp...  13.3 us
    dot_general x2, local copies, waits for them, and re-layouts, cross_spectra(): jnp.einsum('wsf,wrf->rsf', src_imag, rec_real, preferred_element_type=jnp...  13.3 us
  transfers between devices with their start and end apart: 3, of which 3 were waited for; matrix products, arithmetic and copies ran while one was open for 21% of the time, Pallas kernels for 0%

commit v1 on v0

--- a/solution.py
+++ b/solution.py
@@ -11,7 +11,7 @@
 
 def from_root(value, axis, source):
     kept = jnp.where(lax.axis_index(axis) == source, value, 0).astype(value.dtype)
-    return lax.psum(kept, axis)
+    return jnp.sum(lax.all_gather(kept, axis), axis=0)
 
 
 def lag_table(bins, lags, factor):

time: 445 us -> 365 us (0.82)
  waiting for transfers between devices: 257 us -> 166 us
  other arithmetic: 33.3 us -> 41.6 us
  matrix products: 63.9 us -> 68.8 us
    psum x1 -> x0, waiting for transfers between devices: 136 us -> none  [from_root(): return lax.psum(kept, axis)]
    all_gather x0 -> x2, waiting for transfers between devices: none -> 57.3 us  [from_root(): return jnp.sum(lax.all_gather(kept, axis), axis=0)]
    reduce_scatter x2, waiting for transfers between devices: 121 us -> 108 us  [body(): lax.psum_scatter(partial_cross, 'win', scatter_dimension=0, tiled=True)]
    sub x2, other arithmetic: 0.5 us -> 7.87 us  [cross_spectra(): imag_part - jnp.einsum('wsf,wrf->rsf', src_imag, rec_real, preferred_elem...]
    reduce_sum x0 -> x2, other arithmetic: none -> 5.97 us  [from_root(): return jnp.sum(lax.all_gather(kept, axis), axis=0)]
    add x2 -> x0, other arithmetic: 4.68 us -> none  [cross_spectra(): real_part + jnp.einsum('wsf,wrf->rsf', src_imag, rec_imag, preferred_elem...]
  transfers between devices with their start and end apart: 3 -> 4, of which waited for: 3 -> 3; matrix products, arithmetic and copies ran while one was open for 21% -> 45% of each run, Pallas kernels for 0% -> 0%
where the time goes in v1:
time: 365 us; the launch traced here: 364 us
  waiting for transfers between devices  166 us (45%)
  matrix products  68.8 us (19%)
  local copies, waits for them, and re-layouts  68.7 us (19%)
  other arithmetic  41.6 us (11%)
  between operations  18.6 us (5%)
    reduce_scatter x2, waiting for transfers between devices, body(): lax.psum_scatter(partial_cross, 'win', scatter_dimension=0, tiled=True)  108 us
    all_gather x2, waiting for transfers between devices, from_root(): return jnp.sum(lax.all_gather(kept, axis), axis=0)  57.3 us
    cos x1, other arithmetic, lag_table(): jnp.cos(phase_angle)  18 us
    dot_general x2, matrix products, apply_lags(): jnp.dot(cross.reshape(-1, cross.shape[-1]), transform, precision=lax.Prec...  15.6 us
    dot_general x2, matrix products, cross_spectra(): jnp.einsum('wsf,wrf->rsf', src_imag, rec_real, preferred_element_type=jnp...  14.6 us
    dot_general x2, matrix products, cross_spectra(): jnp.einsum('wsf,wrf->rsf', src_real, rec_real, preferred_element_type=jnp...  14.5 us
    dot_general x2, local copies, waits for them, and re-layouts, cross_spectra(): jnp.einsum('wsf,wrf->rsf', src_real, rec_imag, preferred_element_type=jnp...  13.5 us
    dot_general x2, local copies, waits for them, and re-layouts, cross_spectra(): jnp.einsum('wsf,wrf->rsf', src_imag, rec_imag, preferred_element_type=jnp...  13.4 us
  transfers between devices with their start and end apart: 4, of which 3 were waited for; matrix products, arithmetic and copies ran while one was open for 45% of the time, Pallas kernels for 0%

profile of v1, /device:TPU:8, one launch (start us, length us, event | category | flops | bytes accessed | tf_op | source)
XLA Modules:
  0.0 364.2 jit_solution(15475940115260367823)
XLA Ops:
  20.2 2.5 copy.4
  22.7 57.3 %all-gather.5.cloned.1.call-done = bf16[64,8,4096]{2,1,0:T(8,128)(2,1)} async-done(((bf16[4,8,4096]{2,1,0:T(8,128)(2,1)}), bf16[64,8,4096]{2,1,0:T(8,128)(2,1)}) %all-gather.5.cloned.1.call-update) | async-done | bytes 4194320 | tf_op jit(solution)/shard_map/all_gather | solution.py:14
  80.0 3.0 reduce_sum.34
  83.0 2.4 copy.5
  85.5 6.0 %fusion.38 = f32[2048,32,8]{1,2,0:T(8,128)} fusion(bf16[4,32,2048]{1,0,2:T(4,128)(2,1)S(1)} %copy.7, bf16[4,8,2048]{1,0,2:T(4,128)(2,1)} %copy.5), kind=kOutput, calls=%fused_computation.46 | convolution fusion | flops 4194304 | bytes 2752512 | tf_op jit(solution)/shard_map/wsf,wrf->rsf/dot_general | solution.py:43
  91.5 6.7 %copy.10 = f32[2048,32,8]{0,2,1:T(8,128)} copy(f32[2048,32,8]{1,2,0:T(8,128)} %fusion.38) | data formatting | bytes 4194304 | tf_op jit(solution)/shard_map/wsf,wrf->rsf/dot_general | solution.py:43
  98.2 2.4 copy.8
  100.6 7.3 %fusion.39 = f32[2048,32,8]{1,2,0:T(8,128)} fusion(bf16[4,32,2048]{1,0,2:T(4,128)(2,1)} %copy.4, bf16[4,8,2048]{1,0,2:T(4,128)(2,1)} %copy.8), kind=kOutput, calls=%fused_computation.47 | convolution fusion | flops 4194304 | bytes 2752512 | tf_op jit(solution)/shard_map/wsf,wrf->rsf/dot_general | solution.py:44
  107.9 6.6 %copy.11 = f32[2048,32,8]{0,2,1:T(8,128)} copy(f32[2048,32,8]{1,2,0:T(8,128)} %fusion.39) | data formatting | bytes 4194304 | tf_op jit(solution)/shard_map/wsf,wrf->rsf/dot_general | solution.py:44
  114.5 7.2 %fusion.36 = f32[2048,32,8]{1,2,0:T(8,128)} fusion(bf16[4,32,2048]{1,0,2:T(4,128)(2,1)} %copy.4, bf16[4,8,2048]{1,0,2:T(4,128)(2,1)} %copy.5), kind=kOutput, calls=%fused_computation.44 | convolution fusion | flops 4194304 | bytes 2752512 | tf_op jit(solution)/shard_map/wsf,wrf->rsf/dot_general | solution.py:39
  121.8 6.6 %copy.6 = f32[2048,32,8]{0,2,1:T(8,128)} copy(f32[2048,32,8]{1,2,0:T(8,128)} %fusion.36) | data formatting | bytes 4194304 | tf_op jit(solution)/shard_map/wsf,wrf->rsf/dot_general | solution.py:39
  128.4 6.0 %fusion.37 = f32[2048,32,8]{1,2,0:T(8,128)} fusion(bf16[4,32,2048]{1,0,2:T(4,128)(2,1)S(1)} %copy.7, bf16[4,8,2048]{1,0,2:T(4,128)(2,1)} %copy.8), kind=kOutput, calls=%fused_computation.45 | convolution fusion | flops 4194304 | bytes 2752512 | tf_op jit(solution)/shard_map/wsf,wrf->rsf/dot_general | solution.py:40
  134.5 6.8 %copy.9 = f32[2048,32,8]{0,2,1:T(8,128)} copy(f32[2048,32,8]{1,2,0:T(8,128)} %fusion.37) | data formatting | bytes 4194304 | tf_op jit(solution)/shard_map/wsf,wrf->rsf/dot_general | solution.py:40
  141.2 4.2 %subtract_bitcast_fusion.1 = (f32[32,8,2048]{2,1,0:T(8,128)S(1)}, f32[32,8,2048]{2,1,0:T(8,128)S(1)}) fusion(f32[2048,32,8]{0,2,1:T(8,128)} %copy.10, f32[2048,32,8]{0,2,1:T(8,128)} %copy.11, f32[2048,32,8]{0,2,1:T(8,128)} %copy.6, f32[2048,32,8]{0,2,1:T(8,128)} %copy.9), kind=kLoop, calls=%fused_computation.25 | loop fusion | flops 1048576 | bytes 12582912 | tf_op jit(solution)/shard_map/sub | solution.py:44
  145.5 2.3 pad_maximum_fusion
  148.0 3.0 reduce_sum.35
  151.0 2.5 copy.12
  153.5 7.2 %fusion.40 = f32[2048,32,8]{1,2,0:T(8,128)} fusion(bf16[4,32,2048]{1,0,2:T(4,128)(2,1)} %copy.4, bf16[4,8,2048]{1,0,2:T(4,128)(2,1)} %copy.12), kind=kOutput, calls=%fused_computation.48 | convolution fusion | flops 4194304 | bytes 2752512 | tf_op jit(solution)/shard_map/wsf,wrf->rsf/dot_general | solution.py:39
  160.7 6.6 %copy.13 = f32[2048,32,8]{0,2,1:T(8,128)} copy(f32[2048,32,8]{1,2,0:T(8,128)} %fusion.40) | data formatting | bytes 4194304 | tf_op jit(solution)/shard_map/wsf,wrf->rsf/dot_general | solution.py:39
  167.4 2.4 copy.14
  169.8 6.1 %fusion.41 = f32[2048,32,8]{1,2,0:T(8,128)} fusion(bf16[4,32,2048]{1,0,2:T(4,128)(2,1)S(1)} %copy.7, bf16[4,8,2048]{1,0,2:T(4,128)(2,1)} %copy.14), kind=kOutput, calls=%fused_computation.49 | convolution fusion | flops 4194304 | bytes 2752512 | tf_op jit(solution)/shard_map/wsf,wrf->rsf/dot_general | solution.py:40
  175.9 6.7 %copy.15 = f32[2048,32,8]{0,2,1:T(8,128)} copy(f32[2048,32,8]{1,2,0:T(8,128)} %fusion.41) | data formatting | bytes 4194304 | tf_op jit(solution)/shard_map/wsf,wrf->rsf/dot_general | solution.py:40
  182.5 7.3 %fusion.43 = f32[2048,32,8]{1,2,0:T(8,128)} fusion(bf16[4,32,2048]{1,0,2:T(4,128)(2,1)} %copy.4, bf16[4,8,2048]{1,0,2:T(4,128)(2,1)} %copy.14), kind=kOutput, calls=%fused_computation.51 | convolution fusion | flops 4194304 | bytes 2752512 | tf_op jit(solution)/shard_map/wsf,wrf->rsf/dot_general | solution.py:44
  189.8 6.7 %copy.17 = f32[2048,32,8]{0,2,1:T(8,128)} copy(f32[2048,32,8]{1,2,0:T(8,128)} %fusion.43) | data formatting | bytes 4194304 | tf_op jit(solution)/shard_map/wsf,wrf->rsf/dot_general | solution.py:44
  196.5 6.1 %fusion.42 = f32[2048,32,8]{1,2,0:T(8,128)} fusion(bf16[4,32,2048]{1,0,2:T(4,128)(2,1)S(1)} %copy.7, bf16[4,8,2048]{1,0,2:T(4,128)(2,1)} %copy.12), kind=kOutput, calls=%fused_computation.50 | convolution fusion | flops 4194304 | bytes 2752512 | tf_op jit(solution)/shard_map/wsf,wrf->rsf/dot_general | solution.py:43
  202.5 6.8 %copy.16 = f32[2048,32,8]{0,2,1:T(8,128)} copy(f32[2048,32,8]{1,2,0:T(8,128)} %fusion.42) | data formatting | bytes 4194304 | tf_op jit(solution)/shard_map/wsf,wrf->rsf/dot_general | solution.py:43
  209.3 3.6 %subtract_bitcast_fusion = (f32[32,8,2048]{2,1,0:T(8,128)S(1)}, f32[32,8,2048]{2,1,0:T(8,128)S(1)}) fusion(f32[2048,32,8]{0,2,1:T(8,128)} %copy.16, f32[2048,32,8]{0,2,1:T(8,128)} %copy.17, f32[2048,32,8]{0,2,1:T(8,128)S(1)} %copy-done, f32[2048,32,8]{0,2,1:T(8,128)} %copy.15), kind=kLoop, calls=%fused_computation.22 | loop fusion | flops 1048576 | bytes 12582912 | tf_op jit(solution)/shard_map/sub | solution.py:44
  215.3 18.0 %fusion.15 = (f32[2048,512]{1,0:T(8,128)}, f32[2048,512]{1,0:T(8,128)}) fusion(s32[512]{0:T(512)S(1)} %iota_add_fusion), kind=kLoop, calls=%fused_computation.24 | loop fusion | flops 15728640 | bytes 8390656 | tf_op jit(solution)/shard_map/cos | solution.py:22
  233.3 13.9 %reduce-scatter.3.cloned.1.call-done = f32[2,8,4096]{2,1,0:T(8,128)} async-done(((f32[32,8,4096]{2,1,0:T(8,128)}), f32[2,8,4096]{2,1,0:T(8,128)}) %reduce-scatter.3.cloned.1.call-update) | async-done | bytes 262160 | tf_op jit(solution)/shard_map/reduce_scatter | solution.py:75
  247.2 7.8 %fusion.25 = bf16[1,2,8,512]{3,2,1,0:T(8,128)(2,1)S(1)} fusion(f32[2,8,4096]{2,1,0:T(8,128)} %reduce-scatter.3.cloned.1.call-done, f32[2048,512]{1,0:T(8,128)} %get-tuple-element.14, f32[2048,512]{1,0:T(8,128)} %get-tuple-element.13), kind=kOutput, calls=%fused_computation.30 | convolution fusion | flops 406855680 | bytes 8667136 | tf_op jit(solution)/shard_map/dot_general | solution.py:51
  255.0 94.3 %reduce-scatter.5.cloned.1.call-done = f32[2,8,4096]{2,1,0:T(8,128)} async-done(((f32[32,8,4096]{2,1,0:T(8,128)}), f32[2,8,4096]{2,1,0:T(8,128)}) %reduce-scatter.5.cloned.1.call-update) | async-done | bytes 262160 | tf_op jit(solution)/shard_map/reduce_scatter | solution.py:75
  349.3 7.8 %fusion.22 = bf16[1,2,8,512]{3,2,1,0:T(8,128)(2,1)S(1)} fusion(f32[2,8,4096]{2,1,0:T(8,128)} %reduce-scatter.5.cloned.1.call-done, f32[2048,512]{1,0:T(8,128)} %get-tuple-element.14, f32[2048,512]{1,0:T(8,128)} %get-tuple-element.13), kind=kOutput, calls=%fused_computation.29 | convolution fusion | flops 406855680 | bytes 8667136 | tf_op jit(solution)/shard_map/dot_general | solution.py:51
  (24 shorter events, 11.4 us)
Async XLA Ops:
  6.5 73.5 %all-gather.5.cloned.1.call-start = ((), (), s32[]{:S(2)}) async-start(), calls=%async_computation.4 | async-start | bytes 4456448 | tf_op jit(solution)/shard_map/all_gather | solution.py:14
  17.9 130.1 %all-gather.7.cloned.1.call-start = ((), (), s32[]{:S(2)}) async-start(), calls=%async_computation.5 | async-start | bytes 4456448 | tf_op jit(solution)/shard_map/all_gather | solution.py:14
  18.7 228.5 %reduce-scatter.3.cloned.1.call-start = ((), (), s32[]{:S(2)}) async-start(), calls=%async_computation.2 | async-start | bytes 4456448 | tf_op jit(solution)/shard_map/reduce_scatter | solution.py:75
  147.8 201.5 %reduce-scatter.5.cloned.1.call-start = ((), (), s32[]{:S(2)}) async-start(), calls=%async_computation.3 | async-start | bytes 4456448 | tf_op jit(solution)/shard_map/reduce_scatter | solution.py:75
  202.5 6.8 %copy-start = (f32[2048,32,8]{0,2,1:T(8,128)S(1)}, f32[2048,32,8]{0,2,1:T(8,128)}, u32[]{:S(2)}) copy-start(f32[2048,32,8]{0,2,1:T(8,128)} %copy.13) | copy-start | bytes 6291460
Sparse Core Ops, SparseCore 0:
  18.1 61.9 all-gather.4
  82.8 58.2 all-gather.6
  147.9 99.2 reduce-scatter.2
  249.6 99.6 reduce-scatter.4
